TPU v7x, 256 devices: a whole 4x4x8 slice. The times are simulated.
256 devices in a mesh: tile: 64 (over y, x_hi, z), rcpt: 4 (over x_lo, core).
Axes of the slice: x: 4 (x_hi: 2, x_lo: 2; x = x_hi * 2 + x_lo), y: 4, z: 8, core: 2. Of those that a mesh axis runs over, the one named last changes fastest.
Arguments:
- adjoint_state: float32 [64, 16, 1024, 256], P('rcpt', None, 'tile'), may hold values from -6 to 6
- met_fields: bfloat16 [12, 3, 16, 1024, 256], P(None, None, 'rcpt', 'tile'), may hold values from -0.34960938 to 0.34960938
- forcing: bfloat16 [64, 1024, 256], P(None, 'tile'), may hold values from -6 to 6
- cluster_ids: int32 [64], P('rcpt'), may hold values from 0 to 63
- hour_index: int32 [2], replicated, may hold values from 0 to 11
Outputs:
- adjoint_out: float32 [64, 16, 1024, 256], P('rcpt', None, 'tile')
All inputs are finite; a program needn't handle non-finite values.
Results may differ from a plain program's by a relative error of at most 0.00035.
Values may be sent and summed in bfloat16 or wider, within the bound.
No kernel may reach another device: no remote copies, remote signals or barrier semaphores. Data moves between devices by JAX's collectives and lax.ppermute only.
A program may use at most 64 MiB of HBM per device.

v0:
```python
import jax
import jax.numpy as jnp
from jax import lax
from jax.sharding import PartitionSpec as P

STEPS = 2


def for_sending(x):

    def short(part):
        return part.astype(jnp.bfloat16) if part.dtype == jnp.float32 else part

    return jax.tree.map(short, x)


def passed_along(block, axis, distance):
    devices = range(lax.axis_size(axis))
    route = [((i - distance) % len(devices), i) for i in devices]
    return lax.ppermute(block, axis, route)


def interior(lam, winds, east, west):
    cx = winds[0].astype(jnp.float32)
    cy = winds[1].astype(jnp.float32)
    py = lam * jnp.maximum(cy, 0.0)
    my = lam * jnp.minimum(cy, 0.0)
    zero = jnp.zeros_like(py[..., :1])
    north = jnp.concatenate([py[..., 1:], zero], axis=3)
    south = jnp.concatenate([zero, my[..., :-1]], axis=3)
    return lam * (1.0 - jnp.abs(cx) - jnp.abs(cy)) + east - west + north - south


def horizontal_shift(lam, winds):
    cx = winds[0].astype(jnp.float32)
    px = lam * jnp.maximum(cx, 0.0)
    mx = lam * jnp.minimum(cx, 0.0)
    east_edge = passed_along(for_sending(px[:, :, :1]), "tile", -1)
    west_edge = passed_along(for_sending(mx[:, :, -1:]), "tile", 1)
    east = jnp.concatenate([px[:, :, 1:], east_edge], axis=2)
    west = jnp.concatenate([west_edge, mx[:, :, :-1]], axis=2)
    return interior(lam, winds, east, west)


def vertical(lam, mixing):
    coeff = 0.02 + 0.25 * jnp.abs(mixing.astype(jnp.float32))
    flux = coeff[:-1] * (lam[:, 1:] - lam[:, :-1])
    zero = jnp.zeros_like(flux[:, :1])
    return jnp.concatenate([flux, zero], axis=1) - jnp.concatenate([zero, flux], axis=1)


def finish(lam, flat, mixing, source_rows):
    state = flat + vertical(lam, mixing)
    return state.at[:, -1].add(source_rows)


def per_device(adjoint_state, met_fields, forcing, cluster_ids, hour_index):
    lam = adjoint_state
    clusters = forcing.shape[0]
    onehot = (cluster_ids[:, None] == jnp.arange(clusters, dtype=jnp.int32)[None, :]).astype(
        jnp.bfloat16
    )
    source_rows = jnp.dot(onehot, forcing.reshape(clusters, -1), preferred_element_type=jnp.float32)
    source_rows = source_rows.reshape(lam.shape[0], lam.shape[2], lam.shape[3])
    locals_list = [
        lax.dynamic_index_in_dim(met_fields, hour_index[step], 0, keepdims=False)
        for step in range(STEPS)
    ]
    for step in range(STEPS):
        metnow = lax.all_gather(locals_list[step], "rcpt", axis=1, tiled=True)
        lam_next = finish(lam, horizontal_shift(lam, metnow), metnow[2], source_rows)
        lam = lam_next
    return lam


def solution(mesh):
    placed = (
        P("rcpt", None, "tile", None),
        P(None, None, "rcpt", "tile", None),
        P(None, "tile", None),
        P("rcpt"),
        P(),
    )
    return jax.shard_map(
        per_device,
        mesh=mesh,
        in_specs=placed,
        out_specs=P("rcpt", None, "tile", None),
        check_vma=False,
    )
```

profile of v0, /device:TPU:1, one launch (start us, length us, event | category | flops | bytes accessed | tf_op | source)
XLA Modules:
  0.0 97.3 jit_solution(4686769854852998408)
XLA Ops:
  0.0 1.3 %fusion.32 = (s32[1]{0:T(128)}, s32[1]{0:T(128)}) fusion(s32[2]{0:T(128)} %param.13), kind=kLoop, calls=%fused_computation.69 | loop fusion | bytes 16 | tf_op jit(solution)/shard_map/slice | solution.py:66
  4.9 1.0 constant_dynamic-slice_fusion
  5.9 9.2 %all-gather = bf16[1,3,16,16,256]{4,3,2,1,0:T(8,128)(2,1)S(1)} all-gather(bf16[1,3,4,16,256]{4,3,2,1,0:T(8,128)(2,1)S(1)} %get-tuple-element.39), channel_id=2, replica_groups=mesh['tile'=64,'rcpt'=4] {'rcpt'}, dimensions={2}, use_global_device_ids=true | all-gather | bytes 491520 | tf_op jit(solution)/shard_map/all_gather | solution.py:70
  15.3 6.5 %fusion.31 = (f32[16,16,16,256]{3,0,2,1:T(8,128)S(1)}, f32[16,16,16,256]{3,0,2,1:T(8,128)S(1)}, f32[16,16,16,256]{3,0,2,1:T(8,128)S(1)}) fusion(f32[16,16,16,256]{3,2,1,0:T(8,128)} %param.9, f32[16,16,256]{2,1,0:T(8,128)S(1)} %get-tuple-element.47, f32[16,16,256]{2,1,0:T(8,128)S(1)} %get-tuple-element.50), kind=kLoop, calls=%fused_computation.68 | loop fusion | flops 2097152 | bytes 17301504 | tf_op args[0]
  21.8 0.7 slice.250
  22.7 0.7 slice.251
  23.4 8.6 %collective-permute-start = (bf16[16,16,1,256]{3,0,2,1:T(8,128)(2,1)}, bf16[16,16,1,256]{3,0,2,1:T(8,128)(2,1)}, u32[]{:S(2)}, u32[]{:S(2)}) collective-permute-start(bf16[16,16,1,256]{3,0,2,1:T(8,128)(2,1)} %slice.251), channel_id=1, source_target_pairs={{4,0},{8,4},{12,8},{16,12},{20,16},{24,20},{28,24},{32,28},{36,32}... | collective-permute-start | bytes 393224 | tf_op jit(solution)/shard_map/ppermute | solution.py:20
  32.0 2.3 %slice.182 = f32[16,16,15,256]{3,0,2,1:T(8,128)} slice(f32[16,16,16,256]{3,0,2,1:T(8,128)S(1)} %get-tuple-element.36), slice={[0:16], [0:16], [1:16], [0:256]} | slice | bytes 7864320 | tf_op jit(solution)/shard_map/slice | solution.py:40
  34.3 2.3 %slice.185 = f32[16,16,15,256]{3,0,2,1:T(8,128)} slice(f32[16,16,16,256]{3,0,2,1:T(8,128)S(1)} %get-tuple-element.37), slice={[0:16], [0:16], [0:15], [0:256]} | slice | bytes 7864320 | tf_op jit(solution)/shard_map/slice | solution.py:41
  36.6 6.7 %all-gather.1 = bf16[1,3,16,16,256]{4,3,2,1,0:T(8,128)(2,1)S(1)} all-gather(bf16[1,3,4,16,256]{4,3,2,1,0:T(8,128)(2,1)S(1)} %get-tuple-element.38), channel_id=3, replica_groups=mesh['tile'=64,'rcpt'=4] {'rcpt'}, dimensions={2}, use_global_device_ids=true | all-gather | bytes 491520 | tf_op jit(solution)/shard_map/all_gather | solution.py:70
  43.4 0.8 slice.187
  44.2 1.0 fusion.22
  45.2 0.9 slice.202
  46.1 2.5 %fusion.9 = f32[16,15,16,256]{3,0,2,1:T(8,128)} fusion(f32[16,16,16,256]{3,0,2,1:T(8,128)S(1)} %get-tuple-element.35, f32[15,16,256]{2,1,0:T(8,128)S(1)} %slice_bitcast_fusion.1), kind=kLoop, calls=%fused_computation.17 | loop fusion | flops 1966080 | bytes 12042240 | tf_op jit(solution)/shard_map/mul | solution.py:47
  48.6 3.0 %slice_multiply_fusion.3 = (f32[16,16,16,255]{3,0,2,1:T(8,128)S(1)}, f32[16,16,16,255]{3,0,2,1:T(8,128)S(1)}) fusion(f32[16,16,16,256]{3,0,2,1:T(8,128)S(1)} %get-tuple-element.35, f32[16,16,255]{2,1,0:T(8,128)} %slice.187, f32[16,16,255]{2,1,0:T(8,128)S(1)} %bitcast.53), kind=kLoop, calls=%fused_computation.3 | loop fusion | flops 2088960 | bytes 17233920 | tf_op jit(solution)/shard_map/mul | solution.py:26
  51.6 1.7 %slice_bitcast_fusion = f32[15,16,256]{2,1,0:T(8,128)} fusion(f32[1,16,16,256]{3,2,1,0:T(8,128)} %get-tuple-element.45), kind=kLoop, calls=%fused_computation.61 | loop fusion | bytes 491520 | tf_op jit(solution)/shard_map/slice | solution.py:47
  53.2 0.9 convert_element_type.54
  54.2 0.9 convert_element_type.53
  55.2 12.0 %fusion.3 = f32[16,16,16,256]{3,0,2,1:T(8,128)S(1)} fusion(f32[16,16,1,256]{3,0,2,1:T(8,128)S(1)} %convert_element_type.53, f32[16,16,15,256]{3,0,2,1:T(8,128)} %slice.182, f32[16,16,15,256]{3,0,2,1:T(8,128)} %slice.185, f32[16,16,1,256]{3,0,2,1:T(8,128)S(1)} %convert_element_type.54, f32[16,15,16,256]{3,0,2,1:T(8,128)} %fusion.9, ...), kind=kLoop, calls=%fused_computation.8 | loop fusion | flops 9437184 | bytes 29327360 | tf_op jit(solution)/shard_map/add | solution.py:53
  67.2 0.3 fusion.27
  67.5 0.9 broadcast_multiply_fusion
  68.4 0.7 slice.248
  69.1 1.2 %slice.249 = bf16[16,16,1,256]{3,0,2,1:T(8,128)(2,1)} slice(f32[16,16,16,256]{3,0,2,1:T(8,128)S(1)} %get-tuple-element.32), slice={[0:16], [0:16], [0:1], [0:256]} | slice | bytes 262144 | tf_op jit(solution)/shard_map/slice | solution.py:38
  70.3 1.6 %collective-permute-start.2 = (bf16[16,16,1,256]{3,0,2,1:T(8,128)(2,1)}, bf16[16,16,1,256]{3,0,2,1:T(8,128)(2,1)}, u32[]{:S(2)}, u32[]{:S(2)}) collective-permute-start(bf16[16,16,1,256]{3,0,2,1:T(8,128)(2,1)} %slice.249), channel_id=1, source_target_pairs={{4,0},{8,4},{12,8},{16,12},{20,16},{24,20},{28,24},{32,28},{36,32}... | collective-permute-start | bytes 393224 | tf_op jit(solution)/shard_map/ppermute | solution.py:20
  71.9 1.8 %slice_multiply_fusion.1 = (f32[16,16,16,255]{3,0,2,1:T(8,128)S(1)}, f32[16,16,16,255]{3,0,2,1:T(8,128)S(1)}) fusion(f32[16,16,16,256]{3,0,2,1:T(8,128)S(1)} %get-tuple-element.54, f32[16,16,255]{2,1,0:T(8,128)S(1)} %copy-done.3, f32[16,16,255]{2,1,0:T(8,128)S(1)} %bitcast.52), kind=kLoop, calls=%fused_computation.1 | loop fusion | flops 2088960 | bytes 17233920 | tf_op jit(solution)/shard_map/mul | solution.py:26
  73.7 3.6 %fusion.8 = f32[16,15,16,256]{3,0,2,1:T(8,128)} fusion(f32[16,16,16,256]{3,0,2,1:T(8,128)S(1)} %get-tuple-element.54, f32[15,16,256]{2,1,0:T(8,128)} %slice_bitcast_fusion), kind=kLoop, calls=%fused_computation.15 | loop fusion | flops 1966080 | bytes 12042240 | tf_op jit(solution)/shard_map/mul | solution.py:47
  77.4 2.3 %slice.200 = f32[16,16,15,256]{3,0,2,1:T(8,128)} slice(f32[16,16,16,256]{3,0,2,1:T(8,128)S(1)} %copy-done.2), slice={[0:16], [0:16], [0:15], [0:256]} | slice | bytes 7864320 | tf_op jit(solution)/shard_map/slice | solution.py:41
  79.7 2.3 %slice.197 = f32[16,16,15,256]{3,0,2,1:T(8,128)} slice(f32[16,16,16,256]{3,0,2,1:T(8,128)S(1)} %get-tuple-element.32), slice={[0:16], [0:16], [1:16], [0:256]} | slice | bytes 7864320 | tf_op jit(solution)/shard_map/slice | solution.py:40
  82.0 0.9 convert_element_type.58
  82.9 0.9 convert_element_type.59
  83.9 8.9 %fusion.7 = f32[16,16,16,256]{3,0,2,1:T(8,128)S(1)} fusion(f32[16,16,1,256]{3,0,2,1:T(8,128)S(1)} %convert_element_type.58, f32[16,16,15,256]{3,0,2,1:T(8,128)} %slice.197, f32[16,16,15,256]{3,0,2,1:T(8,128)} %slice.200, f32[16,16,1,256]{3,0,2,1:T(8,128)S(1)} %convert_element_type.59, f32[16,15,16,256]{3,0,2,1:T(8,128)} %fusion.8, ...), kind=kLoop, calls=%fused_computation.13 | loop fusion | flops 9437184 | bytes 29327360 | tf_op jit(solution)/shard_map/add | solution.py:53
  92.8 4.4 %copy.22 = f32[16,16,16,256]{3,2,1,0:T(8,128)} copy(f32[16,16,16,256]{3,0,2,1:T(8,128)S(1)} %fusion.26) | data formatting | bytes 8388608 | tf_op jit(solution)/shard_map/scatter-add | solution.py:54
  (25 shorter events, 0.6 us)
Async XLA Ops:
  22.5 30.7 %collective-permute-start.1 = (bf16[16,16,1,256]{3,0,2,1:T(8,128)(2,1)}, bf16[16,16,1,256]{3,0,2,1:T(8,128)(2,1)}, u32[]{:S(2)}, u32[]{:S(2)}) collective-permute-start(bf16[16,16,1,256]{3,0,2,1:T(8,128)(2,1)} %slice.250), channel_id=1, source_target_pairs={{252,0},{0,4},{4,8},{8,12},{12,16},{16,20},{20,24},{24,28},{28,32}... | collective-permute-start | bytes 393224 | tf_op jit(solution)/shard_map/ppermute | solution.py:20
  23.4 30.7 %collective-permute-start = (bf16[16,16,1,256]{3,0,2,1:T(8,128)(2,1)}, bf16[16,16,1,256]{3,0,2,1:T(8,128)(2,1)}, u32[]{:S(2)}, u32[]{:S(2)}) collective-permute-start(bf16[16,16,1,256]{3,0,2,1:T(8,128)(2,1)} %slice.251), channel_id=1, source_target_pairs={{4,0},{8,4},{12,8},{16,12},{20,16},{24,20},{28,24},{32,28},{36,32}... | collective-permute-start | bytes 393224 | tf_op jit(solution)/shard_map/ppermute | solution.py:20
  48.6 6.5 %copy-start = (f32[16,16,16,256]{3,2,1,0:T(8,128)S(1)}, f32[16,16,16,256]{3,2,1,0:T(8,128)}, u32[]{:S(2)}) copy-start(f32[16,16,16,256]{3,2,1,0:T(8,128)} %param.9) | copy-start | bytes 12582916
  55.1 12.0 %copy-start.6 = (bf16[64,16,256]{2,1,0:T(8,128)(2,1)S(1)}, bf16[64,16,256]{2,1,0:T(8,128)(2,1)}, u32[]{:S(2)}) copy-start(bf16[64,16,256]{2,1,0:T(8,128)(2,1)} %param.11) | copy-start | bytes 1572868
  55.1 12.0 %copy-start.7 = (s32[16]{0:T(128)S(1)}, s32[16]{0:T(128)}, u32[]{:S(2)}) copy-start(s32[16]{0:T(128)} %param.12) | copy-start | bytes 196
  55.1 12.3 %copy-start.4 = (f32[16,16,256]{2,1,0:T(8,128)S(1)}, f32[16,16,256]{2,1,0:T(8,128)}, u32[]{:S(2)}) copy-start(f32[16,16,256]{2,1,0:T(8,128)} %get-tuple-element.41) | copy-start | bytes 786436
  55.2 12.3 %copy-start.5 = (f32[16,16,256]{2,1,0:T(8,128)S(1)}, f32[16,16,256]{2,1,0:T(8,128)}, u32[]{:S(2)}) copy-start(f32[16,16,256]{2,1,0:T(8,128)} %get-tuple-element.44) | copy-start | bytes 786436
  67.5 4.5 %copy-start.3 = (f32[16,16,255]{2,1,0:T(8,128)S(1)}, f32[16,16,255]{2,1,0:T(8,128)}, u32[]{:S(2)}) copy-start(f32[16,16,255]{2,1,0:T(8,128)} %slice.202) | copy-start | bytes 783364
  68.4 3.5 %copy-start.1 = (f32[16,16,16,256]{3,0,2,1:T(8,128)}, f32[16,16,16,256]{3,0,2,1:T(8,128)S(1)}, u32[]{:S(2)}) copy-start(f32[16,16,16,256]{3,0,2,1:T(8,128)S(1)} %get-tuple-element.31) | copy-start | bytes 12582916
  70.3 11.7 %collective-permute-start.2 = (bf16[16,16,1,256]{3,0,2,1:T(8,128)(2,1)}, bf16[16,16,1,256]{3,0,2,1:T(8,128)(2,1)}, u32[]{:S(2)}, u32[]{:S(2)}) collective-permute-start(bf16[16,16,1,256]{3,0,2,1:T(8,128)(2,1)} %slice.249), channel_id=1, source_target_pairs={{4,0},{8,4},{12,8},{16,12},{20,16},{24,20},{28,24},{32,28},{36,32}... | collective-permute-start | bytes 393224 | tf_op jit(solution)/shard_map/ppermute | solution.py:20
  71.9 11.0 %collective-permute-start.3 = (bf16[16,16,1,256]{3,0,2,1:T(8,128)(2,1)}, bf16[16,16,1,256]{3,0,2,1:T(8,128)(2,1)}, u32[]{:S(2)}, u32[]{:S(2)}) collective-permute-start(bf16[16,16,1,256]{3,0,2,1:T(8,128)(2,1)} %slice.248), channel_id=1, source_target_pairs={{252,0},{0,4},{4,8},{8,12},{12,16},{16,20},{20,24},{24,28},{28,32}... | collective-permute-start | bytes 393224 | tf_op jit(solution)/shard_map/ppermute | solution.py:20
  73.7 3.6 %copy-start.2 = (f32[16,16,16,256]{3,0,2,1:T(8,128)S(1)}, f32[16,16,16,256]{3,0,2,1:T(8,128)}, u32[]{:S(2)}) copy-start(f32[16,16,16,256]{3,0,2,1:T(8,128)} %copy-done.1) | copy-start | bytes 12582916
where the time goes:
time: 97.6 us; the launch traced here: 97.3 us
  other arithmetic  44.2 us (45%)
  local copies, waits for them, and re-layouts  22.7 us (23%)
  blocking collectives  15.9 us (16%)
  starting transfers between devices  10.4 us (11%)
  between operations  3.85 us (4%)
    add x2, other arithmetic, finish(): state = flat + vertical(lam, mixing)  20.8 us
    all_gather x2, blocking collectives, per_device(): metnow = lax.all_gather(locals_list[step], 'rcpt', axis=1, tiled=True)  15.9 us
    ppermute x4, starting transfers between devices, passed_along(): return lax.ppermute(block, axis, route)  10.4 us
    unnamed x1, other arithmetic  6.53 us
    mul x2, other arithmetic, vertical(): flux = coeff[:-1] * (lam[:, 1:] - lam[:, :-1])  6.15 us
    mul x2, other arithmetic, interior(): py = lam * jnp.maximum(cy, 0.0)  4.77 us
    slice x2, local copies, waits for them, and re-layouts, horizontal_shift(): east = jnp.concatenate([px[:, :, 1:], east_edge], axis=2)  4.69 us
    slice x2, local copies, waits for them, and re-layouts, horizontal_shift(): west = jnp.concatenate([west_edge, mx[:, :, :-1]], axis=2)  4.56 us
  transfers between devices with their start and end apart: 4, of which 0 were waited for; matrix products, arithmetic and copies ran while one was open for 28% of the time, Pallas kernels for 0%

commit v1 on v0

v1 whole, which is shorter than its diff:
```python
import jax
import jax.numpy as jnp
from jax import lax
from jax.experimental import pallas as pl
from jax.experimental.pallas import tpu as pltpu
from jax.sharding import PartitionSpec as P


BF = jnp.bfloat16
F32 = jnp.float32
SM = pl.BlockSpec(memory_space=pltpu.SMEM)
VM = pl.BlockSpec(memory_space=pltpu.VMEM)
HB = pl.BlockSpec(memory_space=pltpu.HBM)
LN = 128
UP = 8
GR = 40
KP = 17
UN = 2
MIB = 1024 * 1024
DMA = pltpu.SemaphoreType.DMA


def passed_along(block, axis, distance):
    n = lax.axis_size(axis)
    return lax.ppermute(block, axis, [((i - distance) % n, i) for i in range(n)])


def swapped(block, axis, bit):
    return lax.ppermute(block, axis, [(i ^ bit, i) for i in range(lax.axis_size(axis))])


def pack_kernel(hour, ids, lam, met, forcing, own, to_w, to_e, edge_w, edge_e, l0, l1, rows, hs, js, sem, rsem, msem, isem):
    nt, nk, ni, nj = lam.shape
    nb = nj // LN
    ch = 2
    small = [pltpu.make_async_copy(hour, hs, isem.at[0]), pltpu.make_async_copy(ids, js, isem.at[1])]
    copies = [
        [
            pltpu.make_async_copy(
                lam.at[ch * t : ch * t + ch, :, :, b * LN : (b + 1) * LN],
                l0.at[b, ch * t : ch * t + ch, 0:nk, UP : UP + ni, :],
                sem.at[t, b],
            )
            for b in range(nb)
        ]
        for t in range(nt // ch)
    ]
    for c in small + copies[0] + copies[1]:
        c.start()
    for c in small:
        c.wait()
    mcopies = [pltpu.make_async_copy(met.at[hs[s]], own.at[s], msem.at[s]) for s in range(2)]
    rcopies = [pltpu.make_async_copy(forcing.at[js[t]], rows.at[t], rsem.at[t]) for t in range(nt)]
    for c in mcopies + rcopies:
        c.start()
    for cs in copies[2:]:
        for c in cs:
            c.start()
    zero = jnp.zeros((8, LN), F32)

    def clear(t, _):
        for b in range(nb):
            for k in range(nk):
                for ref in (l0, l1):
                    ref[b, t, k, UP - 8 : UP, :] = zero
                    ref[b, t, k, UP + ni : UP + ni + 8, :] = zero
        return 0

    lax.fori_loop(0, nt, clear, 0)
    for c in mcopies:
        c.wait()
    for out, lo, near, far in ((edge_w, 0, 0, 1), (edge_e, ni - 8, ni - 1, ni - 2)):
        for s, f, outs in ((0, 0, ((0, near), (4, far))), (0, 1, ((1, near),)),
                           (0, 2, ((2, near),)), (1, 0, ((3, near),))):
            x = [own[s, f, q, lo : lo + 8, :].astype(F32) for q in range(own.shape[2])]
            for n, c in outs:
                out[n] = jnp.concatenate([y[c - lo : c - lo + 1] for y in x], axis=0).astype(BF)
    for cs, t0 in zip(copies, range(0, nt, ch)):
        for b in range(nb):
            cs[b].wait()
            flat = l0.at[b].reshape(nt * KP * GR, LN)
            for t in range(t0, t0 + ch):
                for out, near, far in ((to_w, 0, 1), (to_e, ni - 1, ni - 2)):
                    for n, c in enumerate((near, far)):
                        x = flat[pl.ds(t * KP * GR + UP + c, nk, stride=GR), :]
                        out[n * nt + t, :, b * LN : (b + 1) * LN] = x.astype(BF)
    for c in rcopies:
        c.wait()
    for t in range(nt):
        r = rows[t].astype(F32)
        to_w[2 * nt, t] = r[0].astype(BF)
        to_e[2 * nt, t] = r[ni - 1].astype(BF)


def pack(hour, ids, lam, met, forcing):
    nt, nk, ni, nj = lam.shape
    nb = nj // LN
    out = jax.ShapeDtypeStruct((2 * nt + 1, nk, nj), BF)
    edge = jax.ShapeDtypeStruct((5, met.shape[2], nj), BF)
    return pl.pallas_call(
        pack_kernel,
        out_shape=[
            jax.ShapeDtypeStruct((2,) + met.shape[1:], BF),
            out,
            out,
            edge,
            edge,
            pltpu.VMEM((nb, nt, KP, GR, LN), F32),
            pltpu.VMEM((nb, nt, KP, GR, LN), F32),
            pltpu.VMEM((nt, ni, nj), BF),
        ],
        in_specs=[HB] * 5,
        out_specs=[VM] * 8,
        scratch_shapes=[
            pltpu.SMEM((2,), jnp.int32), pltpu.SMEM((nt,), jnp.int32),
            DMA((nt // 2, nb)), DMA((nt,)), DMA((2,)), DMA((2,)),
        ],
        compiler_params=pltpu.CompilerParams(vmem_limit_bytes=4 * MIB),
        cost_estimate=pl.CostEstimate(flops=10**6, bytes_accessed=10 * MIB, transcendentals=0),
        name="pack",
    )(hour, ids, lam, met, forcing)


def roll2(x, sh):
    return pltpu.roll(x, sh % LN, 1)


def ends():
    lane = lax.broadcasted_iota(jnp.int32, (8, LN), 1)
    return lane == 0, lane == LN - 1


def shifted(p, o):
    first, last = ends()
    nb = len(p)
    rp = [roll2(x, -1) for x in p]
    ro = [roll2(x, 1) for x in o]
    return [jnp.where(last, rp[(b + 1) % nb], rp[b]) + jnp.where(first, ro[(b - 1) % nb], ro[b]) for b in range(nb)]


def steps_kernel(m0, m1, m2, m3, l0, l1in, rows, res, oc, l1, co, kz):
    ms = (m0, m1, m2, m3)
    _, _, nl, ni, nj = m0.shape
    nb = nj // LN
    nt = rows.shape[0]
    nk = nl * len(ms)
    na = ni // 8
    r = lax.axis_index("rcpt")
    first, last = ends()
    zero = jnp.zeros((8, LN), F32)

    for s in range(2):
        for b in range(nb):
            for a in range(na):
                kz[s, b, 0, 8 * a : 8 * a + 8, :] = zero
            for k in range(nk):
                co[s, 1, b, k, UP + ni : UP + ni + 8, :] = zero
                co[s, 2, b, k, 0:UP, :] = zero
    for m, ref in enumerate(ms):
        base = (r ^ m) * nl

        def coeffs(q, _):
            k = base + q
            top = jnp.where(k < nk - 1, 1.0, 0.0).astype(F32)
            for s in range(2):
                for b in range(nb):
                    for a in range(na):
                        i = 8 * a
                        cx, cy, mx = (ref[s, f, q, i : i + 8, b * LN : (b + 1) * LN].astype(F32) for f in range(3))
                        n = jnp.maximum(cy, 0.0)
                        o = n - cy
                        e = jnp.maximum(cx, 0.0)
                        w = e - cx
                        co[s, 0, b, k, UP + i : UP + i + 8, :] = 1.0 - jnp.abs(cx) - jnp.abs(cy)
                        co[s, 1, b, k, UP + i : UP + i + 8, :] = e
                        co[s, 2, b, k, UP + i : UP + i + 8, :] = w
                        co[s, 3, b, k, UP + i : UP + i + 8, :] = jnp.where(first, 0.0, n) if b == 0 else n
                        co[s, 4, b, k, UP + i : UP + i + 8, :] = jnp.where(last, 0.0, o) if b == nb - 1 else o
                        kz[s, b, k + 1, i : i + 8, :] = (0.02 + 0.25 * jnp.abs(mx)) * top
            return 0

        lax.fori_loop(0, nl, coeffs, 0)

    def run(s, src, put):
        def one(k):
            ku = jnp.minimum(k + 1, nk - 1)
            kd = jnp.maximum(k - 1, 0)
            for a in range(na):
                r0 = UP + 8 * a
                c = []
                for b in range(nb):
                    up = kz[s, b, k + 1, 8 * a : 8 * a + 8, :]
                    dn = kz[s, b, k, 8 * a : 8 * a + 8, :]
                    ce = co[s, 0, b, k, r0 : r0 + 8, :] - up - dn
                    c.append((ce, co[s, 1, b, k, r0 + 1 : r0 + 9, :], co[s, 2, b, k, r0 - 1 : r0 + 7, :], up, dn,
                     co[s, 3, b, k, r0 : r0 + 8, :], co[s, 4, b, k, r0 : r0 + 8, :]))
                for t in range(nt):
                    x = [src[b, t, k, r0 : r0 + 8, :] for b in range(nb)]
                    y = shifted([x[b] * c[b][5] for b in range(nb)], [x[b] * c[b][6] for b in range(nb)])
                    for b in range(nb):
                        ce, ea, we, up, dn, _, _ = c[b]
                        z = ((x[b] * ce + src[b, t, k, r0 + 1 : r0 + 9, :] * ea)
                         + (src[b, t, k, r0 - 1 : r0 + 7, :] * we
                         + src[b, t, ku, r0 : r0 + 8, :] * up)
                         + src[b, t, kd, r0 : r0 + 8, :] * dn) + y[b]
                        put(a, b, t, k, z)

        def body(k, _):
            for u in range(UN):
                one(UN * k + u)
            return 0

        lax.fori_loop(0, nk // UN, body, 0)

    def put1(a, b, t, k, y):
        l1[b, t, k, UP + 8 * a : UP + 8 * a + 8, :] = y

    run(0, l0, put1)
    for t in range(nt):
        x = rows[t].astype(F32)
        for b in range(nb):
            l1[b, t, nk - 1, UP : UP + ni, :] = l1[b, t, nk - 1, UP : UP + ni, :] + x[:, b * LN : (b + 1) * LN]

    def put2(a, b, t, k, y):
        res[b, t, k, 8 * a : 8 * a + 8, :] = y

    run(1, l1, put2)
    for t in range(nt):
        x = rows[t].astype(F32)
        for b in range(nb):
            res[b, t, nk - 1] = res[b, t, nk - 1] + x[:, b * LN : (b + 1) * LN]

    for side, c, out in ((0, ni - 1, 2), (1, 0, 1)):
        for b in range(nb):
            def take(s, f):
                return co.at[s, f, b].reshape(nk * GR, LN)[pl.ds(UP + c, nk, stride=GR), :]

            def mix(d):
                return kz.at[1, b].reshape((nk + 1) * ni, LN)[pl.ds(d * ni + c, nk, stride=ni), :]

            oc[side, 0, b] = take(0, out)
            up, dn = mix(1), mix(0)
            oc[side, 1, b] = take(1, 0) - up - dn
            oc[side, 2, b] = take(1, 2 - side - (1 if side == 0 else -1))
            oc[side, 3, b] = take(1, 3)
            oc[side, 4, b] = take(1, 4)
            oc[side, 5, b] = up
            oc[side, 6, b] = dn


def steps(ms, l0, l1, rows):
    _, _, nl, ni, _ = ms[0].shape
    nb, nt = l0.shape[:2]
    nk = nl * len(ms)
    return pl.pallas_call(
        steps_kernel,
        out_shape=[
            pltpu.VMEM((nb, nt, KP, ni, LN), F32),
            pltpu.VMEM((2, 7, nb, nk, LN), F32),
            pltpu.VMEM(l1.shape, F32),
        ],
        in_specs=[VM] * 7,
        out_specs=[VM] * 3,
        input_output_aliases={5: 2},
        scratch_shapes=[
            pltpu.VMEM((2, 5, nb, nk, GR, LN), F32),
            pltpu.VMEM((2, nb, nk + 1, ni, LN), F32),
        ],
        compiler_params=pltpu.CompilerParams(
            vmem_limit_bytes=12 * MIB),
        cost_estimate=pl.CostEstimate(flops=4 * 10**7, bytes_accessed=20 * MIB, transcendentals=0),
        name="steps",
    )(*ms, l0, l1, rows)[:2]


def finish_kernel(res, l0, oc, from_w, from_e, e0, e1, e2, e3, out, hs, hc, rh, et, osem):
    nb, nt, _, ni, _ = res.shape
    nk = oc.shape[3]
    lanes = lax.broadcasted_iota(jnp.int32, (nk, LN), 1)
    levs = lax.broadcasted_iota(jnp.int32, (nk, LN), 0)
    zero = jnp.zeros((8, LN), F32)
    r = lax.axis_index("rcpt")
    nl = nk // 4
    for m, ref in enumerate((e0, e1, e2, e3)):
        for side in range(2):
            for n in range(5):
                x = ref[side, n].astype(F32)
                for q in range(nl):
                    et[side, n, pl.ds((r ^ m) * nl + q, 1), :] = x[q : q + 1]
    for side, src in ((0, from_e), (1, from_w)):
        sg = 1.0 if side == 0 else -1.0
        for b in range(nb):
            sl = slice(b * LN, (b + 1) * LN)
            hs[side, b, 0:8, :] = zero
            hs[side, b, 8 + nt * nk : 16 + nt * nk, :] = zero
            for t in range(nt):
                hs[side, b, 8 + t * nk : 8 + t * nk + nk, :] = src[t, :, sl].astype(F32)
                rh[side, b, 8 * t : 8 * t + 8, :] = zero
            x = src[2 * nt, :, sl].astype(F32)
            for t in range(nt):
                rh[side, b, 8 * t + 7 : 8 * t + 8, :] = x[t : t + 1]
            cx, cy, m, cx1, far = (et[side, n, :, sl] for n in range(5))
            kk = 0.02 + 0.25 * jnp.abs(m)
            ku = jnp.where(levs == nk - 1, 0.0, kk)
            km = jnp.where(levs == 0, 0.0, pltpu.roll(kk, 1, 0))
            n = jnp.maximum(cy, 0.0)
            o = n - cy
            hc[side, 0, b, 0:nk] = 1.0 - jnp.abs(cx) - jnp.abs(cy) - ku - km
            hc[side, 1, b, 0:nk] = jnp.maximum(sg * far, 0.0)
            hc[side, 2, b, 0:nk] = oc[side, 0, b]
            hc[side, 3, b, 0:nk] = jnp.where(lanes == 0, 0.0, n) if b == 0 else n
            hc[side, 4, b, 0:nk] = jnp.where(lanes == LN - 1, 0.0, o) if b == nb - 1 else o
            hc[side, 5, b, 0:nk] = ku
            hc[side, 6, b, 0:nk] = km
            hc[side, 7, b, 0:8] = zero
            hc[side, 7, b, 8 : 8 + nk] = jnp.maximum(sg * cx, 0.0)
            hc[side, 7, b, 8 + nk : 16 + nk] = zero
            hc[side, 8, b, 0:nk] = jnp.maximum(sg * cx1, 0.0)
    fr = [res.at[b].reshape(nt * KP * ni, LN) for b in range(nb)]
    f0 = [l0.at[b].reshape(nt * KP * GR, LN) for b in range(nb)]

    def one(t, _):
        for side, own, inner in ((0, ni - 1, ni - 2), (1, 0, 1)):
            for h in range(nk // 8):
                k0 = 8 * h
                c = [[hc[side, f, b, k0 : k0 + 8, :] for b in range(nb)] for f in range(7)]
                p = [[oc[side, f, b, k0 : k0 + 8, :] for b in range(nb)] for f in range(7)]
                e = [[hc[side, 7, b, 8 + k0 + d : 16 + k0 + d, :] for b in range(nb)] for d in (-1, 0, 1)]
                ez = [hc[side, 8, b, k0 : k0 + 8, :] for b in range(nb)]
                g = (from_e, from_w)[side]
                x = [[hs[side, b, pl.ds(8 + t * nk + k0 + d, 8), :] for b in range(nb)] for d in (-1, 0, 1)]
                dl = [[x[d][b] * e[d][b] for b in range(nb)] for d in range(3)]
                far = [g[nt + t, k0 : k0 + 8, b * LN : (b + 1) * LN].astype(F32) for b in range(nb)]
                mine = [f0[b][pl.ds((t * KP + k0) * GR + UP + own, 8, stride=GR), :] for b in range(nb)]
                sh = shifted([x[1][b] * c[3][b] for b in range(nb)], [x[1][b] * c[4][b] for b in range(nb)])
                sd = shifted([dl[1][b] * p[3][b] for b in range(nb)], [dl[1][b] * p[4][b] for b in range(nb)])
                for b in range(nb):
                    y = (x[1][b] * c[0][b] + far[b] * c[1][b] + mine[b] * c[2][b] + sh[b]
                         + x[2][b] * c[5][b] + x[0][b] * c[6][b])
                    if h == nk // 8 - 1:
                        y = y + rh[side, b, pl.ds(8 * t, 8), :]
                    z = (y * ez[b] + dl[1][b] * p[1][b] + sd[b]
                         + dl[2][b] * p[5][b] + dl[0][b] * p[6][b])
                    at = pl.ds((t * KP + k0) * ni + own, 8, stride=ni)
                    fr[b][at, :] = fr[b][at, :] + z
                    at = pl.ds((t * KP + k0) * ni + inner, 8, stride=ni)
                    fr[b][at, :] = fr[b][at, :] + dl[1][b] * p[2][b]
        for b in range(nb):
            pltpu.make_async_copy(res.at[b, t, 0:nk], out.at[t, :, :, b * LN : (b + 1) * LN], osem.at[b]).start()
        return 0

    lax.fori_loop(0, nt, one, 0)
    for b in range(nb):
        pltpu.make_async_copy(res.at[b, :, 0:nk], out.at[:, :, :, b * LN : (b + 1) * LN], osem.at[b]).wait()


def finish(res, l0, oc, from_w, from_e, es):
    nb, nt, _, ni, _ = res.shape
    nk = oc.shape[3]
    return pl.pallas_call(
        finish_kernel,
        out_shape=jax.ShapeDtypeStruct((nt, nk, ni, nb * LN), F32),
        in_specs=[VM] * 9,
        out_specs=HB,
        scratch_shapes=[
            pltpu.VMEM((2, nb, 16 + nt * nk, LN), F32),
            pltpu.VMEM((2, 9, nb, 16 + nk, LN), F32),
            pltpu.VMEM((2, nb, 8 * nt, LN), F32),
            pltpu.VMEM((2, 5, nk, nb * LN), F32),
            DMA((nb,)),
        ],
        compiler_params=pltpu.CompilerParams(vmem_limit_bytes=16 * MIB),
        cost_estimate=pl.CostEstimate(flops=10**6, bytes_accessed=8 * MIB, transcendentals=0),
        name="finish",
    )(res, l0, oc, from_w, from_e, *es)


def one_device(*inputs):
    lam, met, src, ids, hour = (pltpu.with_memory_space_constraint(x, pltpu.HBM) for x in inputs)
    own, to_w, to_e, edge_w, edge_e, l0, l1, rows = pack(hour, ids, lam, met, src)
    g2 = swapped(own, "rcpt", 2)
    got_e = passed_along(edge_w, "tile", -1)
    got_w = passed_along(edge_e, "tile", 1)
    from_e = passed_along(to_w, "tile", -1)
    from_w = passed_along(to_e, "tile", 1)
    g1 = swapped(own, "rcpt", 1)
    g3 = swapped(g2, "rcpt", 1)
    e0 = jnp.stack([got_e, got_w])
    es = [e0] + [swapped(e0, "rcpt", m) for m in (1, 2, 3)]
    res, oc = steps((own, g1, g2, g3), l0, l1, rows)
    return finish(res, l0, oc, from_w, from_e, es)


def solution(mesh):
    placed = (
        P("rcpt", None, "tile", None),
        P(None, None, "rcpt", "tile", None),
        P(None, "tile", None),
        P("rcpt"),
        P(),
    )
    return jax.shard_map(
        one_device,
        mesh=mesh,
        in_specs=placed,
        out_specs=P("rcpt", None, "tile", None),
        check_vma=False,
    )
```

time: 97.6 us -> 50.4 us (0.52)
  other arithmetic: 44.2 us -> 0.02 us
  local copies, waits for them, and re-layouts: 22.7 us -> 0 us
  starting transfers between devices: 10.4 us -> 28.3 us
  blocking collectives: 15.9 us -> 0 us
  Pallas kernels: 0 us -> 12.5 us
  waiting for transfers between devices: 0.01 us -> 9.42 us
  between operations: 3.85 us -> 0.07 us
    add x2 -> x0, other arithmetic: 20.8 us -> none  [finish(): state = flat + vertical(lam, mixing)]
    ppermute x4 -> x10, starting transfers between devices: 10.4 us -> 28.3 us  [the longest x4 21.1 us: passed_along(): lax.ppermute(block, axis, [((i - distance) % n, i) for i in range(n)])]
    slice x13 -> x0, local copies, waits for them, and re-layouts: 17.2 us -> none  [the longest x2 4.69 us: horizontal_shift(): east = jnp.concatenate([px[:, :, 1:], east_edge], axis=2)]
    all_gather x2 -> x0, blocking collectives: 15.9 us -> none  [per_device(): metnow = lax.all_gather(locals_list[step], 'rcpt', axis=1, tiled=True)]
    mul x7 -> x0, other arithmetic: 13 us -> none  [the longest x2 6.15 us: vertical(): flux = coeff[:-1] * (lam[:, 1:] - lam[:, :-1])]
    pallas_call x0 -> x3, Pallas kernels: none -> 12.5 us  [the longest x1 6.47 us: steps(): pl.pallas_call(steps_kernel, out_shape=[pltpu.VMEM((nb, nt, KP, ni, LN),...]
    ppermute x4 -> x10, waiting for transfers between devices: 0.01 us -> 9.42 us  [the longest x4 9.41 us: passed_along(): lax.ppermute(block, axis, [((i - distance) % n, i) for i in range(n)])]
    unnamed x1 -> x0, other arithmetic: 6.53 us -> none
  transfers between devices with their start and end apart: 4 -> 10, of which waited for: 0 -> 2; matrix products, arithmetic and copies ran while one was open for 28% -> 0% of each run, Pallas kernels for 0% -> 13%
where the time goes in v1:
time: 50.4 us; the launch traced here: 50.3 us
  starting transfers between devices  28.3 us (56%)
  Pallas kernels  12.5 us (25%)
  waiting for transfers between devices  9.42 us (19%)
    ppermute x4, starting transfers between devices, passed_along(): lax.ppermute(block, axis, [((i - distance) % n, i) for i in range(n)])  21.1 us
    ppermute x4, waiting for transfers between devices, passed_along(): lax.ppermute(block, axis, [((i - distance) % n, i) for i in range(n)])  9.41 us
    ppermute x6, starting transfers between devices, swapped(): lax.ppermute(block, axis, [(i ^ bit, i) for i in range(lax.axis_size(axis...  7.11 us
    pallas_call x1, Pallas kernels, steps(): pl.pallas_call(steps_kernel, out_shape=[pltpu.VMEM((nb, nt, KP, ni, LN),...  6.47 us
    pallas_call x1, Pallas kernels, pack(): pl.pallas_call(pack_kernel, out_shape=[jax.ShapeDtypeStruct((2,) + met.sh...  3.23 us
    pallas_call x1, Pallas kernels, finish(): pl.pallas_call(finish_kernel, out_shape=jax.ShapeDtypeStruct((nt, nk, ni,...  2.81 us
  transfers between devices with their start and end apart: 10, of which 2 were waited for; matrix products, arithmetic and copies ran while one was open for 0% of the time, Pallas kernels for 13%

profile of v1, /device:TPU:1, one launch (start us, length us, event | category | flops | bytes accessed | tf_op | source)
XLA Modules:
  0.0 50.3 jit_solution(14943304321452696997)
XLA Ops:
  0.0 3.2 %pack.1 = (bf16[2,3,4,16,256]{4,3,2,1,0:T(8,128)(2,1)S(1)}, bf16[33,16,256]{2,1,0:T(8,128)(2,1)S(1)}, bf16[33,16,256]{2,1,0:T(8,128)(2,1)S(1)}, bf16[5,4,256]{2,...) custom-call(s32[2]{0:T(128)} %hour.1, s32[16]{0:T(128)} %ids.1, ...), custom_call_target="tpu_custom_call" | custom-call | flops 1000000 | bytes 10485760 | tf_op jit(solution)/shard_map/pack/pallas_call | solution.py:100
  3.2 2.1 %collective-permute-start.1 = (bf16[2,3,4,16,256]{4,3,2,1,0:T(8,128)(2,1)S(1)}, bf16[2,3,4,16,256]{4,3,2,1,0:T(8,128)(2,1)S(1)}, u32[]{:S(2)}, u32[]{:S(2)}) collective-permute-start(bf16[2,3,4,16,256]{4,3,2,1,0:T(8,128)(2,1)S(1)} %get-tuple-element.15.m0), channel_id=1, source_target_pairs={{2,0},{3,1},{0,2},{1,3},{6,4},{7,5},{4,6},{5,7},{10,8},{11,9},{8,1... | collective-permute-start | bytes 589832 | tf_op jit(solution)/shard_map/ppermute | solution.py:29
  5.4 1.6 %collective-permute-start.3 = (bf16[33,16,256]{2,1,0:T(8,128)(2,1)S(1)}, bf16[33,16,256]{2,1,0:T(8,128)(2,1)S(1)}, u32[]{:S(2)}, u32[]{:S(2)}) collective-permute-start(bf16[33,16,256]{2,1,0:T(8,128)(2,1)S(1)} %get-tuple-element.21), channel_id=1, source_target_pairs={{252,0},{0,4},{4,8},{8,12},{12,16},{16,20},{20,24},{24,28},{28,32}... | collective-permute-start | bytes 811016 | tf_op jit(solution)/shard_map/ppermute | solution.py:25
  7.0 8.6 %collective-permute-start.4 = (bf16[33,16,256]{2,1,0:T(8,128)(2,1)S(1)}, bf16[33,16,256]{2,1,0:T(8,128)(2,1)S(1)}, u32[]{:S(2)}, u32[]{:S(2)}) collective-permute-start(bf16[33,16,256]{2,1,0:T(8,128)(2,1)S(1)} %get-tuple-element.22), channel_id=1, source_target_pairs={{4,0},{8,4},{12,8},{16,12},{20,16},{24,20},{28,24},{32,28},{36,32}... | collective-permute-start | bytes 811016 | tf_op jit(solution)/shard_map/ppermute | solution.py:25
  15.6 1.2 %collective-permute-start = (bf16[2,3,4,16,256]{4,3,2,1,0:T(8,128)(2,1)S(1)}, bf16[2,3,4,16,256]{4,3,2,1,0:T(8,128)(2,1)S(1)}, u32[]{:S(2)}, u32[]{:S(2)}) collective-permute-start(bf16[2,3,4,16,256]{4,3,2,1,0:T(8,128)(2,1)S(1)} %get-tuple-element.15.m0), channel_id=1, source_target_pairs={{1,0},{0,1},{3,2},{2,3},{5,4},{4,5},{7,6},{6,7},{9,8},{8,9},{11,10... | collective-permute-start | bytes 589832 | tf_op jit(solution)/shard_map/ppermute | solution.py:29
  16.8 0.0 collective-permute-done.1.m2
  16.8 0.0 collective-permute-start.2
  16.8 10.9 %collective-permute-start.5 = (bf16[5,4,256]{2,1,0:T(4,128)(2,1)S(1)}, bf16[5,4,256]{2,1,0:T(4,128)(2,1)S(1)}, u32[]{:S(2)}, u32[]{:S(2)}) collective-permute-start(bf16[5,4,256]{2,1,0:T(4,128)(2,1)S(1)} %get-tuple-element.23), channel_id=1, source_target_pairs={{4,0},{8,4},{12,8},{16,12},{20,16},{24,20},{28,24},{32,28},{36,32}... | collective-permute-start | bytes 30728 | tf_op jit(solution)/shard_map/ppermute | solution.py:25
  27.7 0.8 %collective-permute-done.5 = bf16[5,4,256]{2,1,0:T(4,128)(2,1)S(1)} collective-permute-done((bf16[5,4,256]{2,1,0:T(4,128)(2,1)S(1)}, bf16[5,4,256]{2,1,0:T(4,128)(2,1)S(1)}, u32[]{:S(2)}, u32[]{:S(2)}) %collective-permute-start.5) | collective-permute-done | bytes 10272 | tf_op jit(solution)/shard_map/ppermute | solution.py:25
  28.6 0.0 collective-permute-start.6
  28.6 8.6 %collective-permute-done.6 = bf16[5,4,256]{2,1,0:T(4,128)(2,1)S(1)} collective-permute-done((bf16[5,4,256]{2,1,0:T(4,128)(2,1)S(1)}, bf16[5,4,256]{2,1,0:T(4,128)(2,1)S(1)}, u32[]{:S(2)}, u32[]{:S(2)}) %collective-permute-start.6) | collective-permute-done | bytes 10272 | tf_op jit(solution)/shard_map/ppermute | solution.py:25
  37.2 2.0 %collective-permute-start.7 = (bf16[2,5,4,256]{3,2,1,0:T(4,128)(2,1)S(1)}, bf16[2,5,4,256]{3,2,1,0:T(4,128)(2,1)S(1)}, u32[]{:S(2)}, u32[]{:S(2)}) collective-permute-start(bf16[2,5,4,256]{3,2,1,0:T(4,128)(2,1)S(1)} %pad_maximum_fusion.e0), channel_id=1, source_target_pairs={{1,0},{0,1},{3,2},{2,3},{5,4},{4,5},{7,6},{6,7},{9,8},{8,9},{11,10... | collective-permute-start | bytes 61448 | tf_op jit(solution)/shard_map/ppermute | solution.py:29
  39.2 0.0 collective-permute-done.m1
  39.2 0.6 %collective-permute-start.8 = (bf16[2,5,4,256]{3,2,1,0:T(4,128)(2,1)S(1)}, bf16[2,5,4,256]{3,2,1,0:T(4,128)(2,1)S(1)}, u32[]{:S(2)}, u32[]{:S(2)}) collective-permute-start(bf16[2,5,4,256]{3,2,1,0:T(4,128)(2,1)S(1)} %pad_maximum_fusion.e0), channel_id=1, source_target_pairs={{2,0},{3,1},{0,2},{1,3},{6,4},{7,5},{4,6},{5,7},{10,8},{11,9},{8,1... | collective-permute-start | bytes 61448 | tf_op jit(solution)/shard_map/ppermute | solution.py:29
  39.8 0.0 collective-permute-done.2.m3
  39.8 1.1 %collective-permute-start.9 = (bf16[2,5,4,256]{3,2,1,0:T(4,128)(2,1)S(1)}, bf16[2,5,4,256]{3,2,1,0:T(4,128)(2,1)S(1)}, u32[]{:S(2)}, u32[]{:S(2)}) collective-permute-start(bf16[2,5,4,256]{3,2,1,0:T(4,128)(2,1)S(1)} %pad_maximum_fusion.e0), channel_id=1, source_target_pairs={{3,0},{2,1},{1,2},{0,3},{7,4},{6,5},{5,6},{4,7},{11,8},{10,9},{9,1... | collective-permute-start | bytes 61448 | tf_op jit(solution)/shard_map/ppermute | solution.py:29
  40.9 6.5 %steps.1 = (f32[2,16,17,16,128]{4,3,2,1,0:T(8,128)S(1)}, f32[2,7,2,16,128]{4,3,2,1,0:T(8,128)S(1)}, f32[2,16,17,40,128]{4,3,2,1,0:T(8,128)S(1)}) custom-call(bf16[2,3,4,16,256]{4,3,2,1,0:T(8,128)(2,1)S(1)} %get-tuple-element.15.m0, bf16[2,3,4,16,256]{4,3,2,1,0:T(8,128)(2,1)S(1)} %collective-permute-done.m1, ...), custom_call_target="tpu_custom_call", output_to_operand_aliasing={{2}: (5, {})} | custom-call | flops 40000000 | bytes 20971520 | tf_op jit(solution)/shard_map/steps/pallas_call | solution.py:255
  47.4 0.0 collective-permute-done.7.e1
  47.4 0.0 collective-permute-done.8.e2
  47.4 0.0 collective-permute-done.9.e3
  47.4 0.0 collective-permute-done.3.from_w
  47.5 0.0 collective-permute-done.4.from_e
  47.5 2.8 %finish.1 = f32[16,16,16,256]{3,2,1,0:T(8,128)} custom-call(f32[2,16,17,16,128]{4,3,2,1,0:T(8,128)S(1)} %get-tuple-element.19.res, f32[2,16,17,40,128]{4,3,2,1,0:T(8,128)S(1)} %get-tuple-element.16.l0, f32[2,7,2,16,128]{4,3,2,1,0:T(8,128)S(1)} %get-tuple-element.20.oc, bf16[33,16,256]{2,1,0:T(8,128)(2,1)S(1)} %collective-permute-done.3.from_w, ...), custom_call_target="tpu_custom_call" | custom-call | flops 1000000 | bytes 8388608 | tf_op jit(solution)/shard_map/finish/pallas_call | solution.py:360
  (1 shorter events, 0.0 us)
Async XLA Ops:
  3.2 13.6 %collective-permute-start.1 = (bf16[2,3,4,16,256]{4,3,2,1,0:T(8,128)(2,1)S(1)}, bf16[2,3,4,16,256]{4,3,2,1,0:T(8,128)(2,1)S(1)}, u32[]{:S(2)}, u32[]{:S(2)}) collective-permute-start(bf16[2,3,4,16,256]{4,3,2,1,0:T(8,128)(2,1)S(1)} %get-tuple-element.15.m0), channel_id=1, source_target_pairs={{2,0},{3,1},{0,2},{1,3},{6,4},{7,5},{4,6},{5,7},{10,8},{11,9},{8,1... | collective-permute-start | bytes 589832 | tf_op jit(solution)/shard_map/ppermute | solution.py:29
  5.4 42.1 %collective-permute-start.3 = (bf16[33,16,256]{2,1,0:T(8,128)(2,1)S(1)}, bf16[33,16,256]{2,1,0:T(8,128)(2,1)S(1)}, u32[]{:S(2)}, u32[]{:S(2)}) collective-permute-start(bf16[33,16,256]{2,1,0:T(8,128)(2,1)S(1)} %get-tuple-element.21), channel_id=1, source_target_pairs={{252,0},{0,4},{4,8},{8,12},{12,16},{16,20},{20,24},{24,28},{28,32}... | collective-permute-start | bytes 811016 | tf_op jit(solution)/shard_map/ppermute | solution.py:25
  7.0 40.5 %collective-permute-start.4 = (bf16[33,16,256]{2,1,0:T(8,128)(2,1)S(1)}, bf16[33,16,256]{2,1,0:T(8,128)(2,1)S(1)}, u32[]{:S(2)}, u32[]{:S(2)}) collective-permute-start(bf16[33,16,256]{2,1,0:T(8,128)(2,1)S(1)} %get-tuple-element.22), channel_id=1, source_target_pairs={{4,0},{8,4},{12,8},{16,12},{20,16},{24,20},{28,24},{32,28},{36,32}... | collective-permute-start | bytes 811016 | tf_op jit(solution)/shard_map/ppermute | solution.py:25
  15.6 23.6 %collective-permute-start = (bf16[2,3,4,16,256]{4,3,2,1,0:T(8,128)(2,1)S(1)}, bf16[2,3,4,16,256]{4,3,2,1,0:T(8,128)(2,1)S(1)}, u32[]{:S(2)}, u32[]{:S(2)}) collective-permute-start(bf16[2,3,4,16,256]{4,3,2,1,0:T(8,128)(2,1)S(1)} %get-tuple-element.15.m0), channel_id=1, source_target_pairs={{1,0},{0,1},{3,2},{2,3},{5,4},{4,5},{7,6},{6,7},{9,8},{8,9},{11,10... | collective-permute-start | bytes 589832 | tf_op jit(solution)/shard_map/ppermute | solution.py:29
  16.8 23.0 %collective-permute-start.2 = (bf16[2,3,4,16,256]{4,3,2,1,0:T(8,128)(2,1)S(1)}, bf16[2,3,4,16,256]{4,3,2,1,0:T(8,128)(2,1)S(1)}, u32[]{:S(2)}, u32[]{:S(2)}) collective-permute-start(bf16[2,3,4,16,256]{4,3,2,1,0:T(8,128)(2,1)S(1)} %collective-permute-done.1.m2), channel_id=1, source_target_pairs={{1,0},{0,1},{3,2},{2,3},{5,4},{4,5},{7,6},{6,7},{9,8},{8,9},{11,10... | collective-permute-start | bytes 589832 | tf_op jit(solution)/shard_map/ppermute | solution.py:29
  16.8 11.8 %collective-permute-start.5 = (bf16[5,4,256]{2,1,0:T(4,128)(2,1)S(1)}, bf16[5,4,256]{2,1,0:T(4,128)(2,1)S(1)}, u32[]{:S(2)}, u32[]{:S(2)}) collective-permute-start(bf16[5,4,256]{2,1,0:T(4,128)(2,1)S(1)} %get-tuple-element.23), channel_id=1, source_target_pairs={{4,0},{8,4},{12,8},{16,12},{20,16},{24,20},{28,24},{32,28},{36,32}... | collective-permute-start | bytes 30728 | tf_op jit(solution)/shard_map/ppermute | solution.py:25
  28.6 8.6 %collective-permute-start.6 = (bf16[5,4,256]{2,1,0:T(4,128)(2,1)S(1)}, bf16[5,4,256]{2,1,0:T(4,128)(2,1)S(1)}, u32[]{:S(2)}, u32[]{:S(2)}) collective-permute-start(bf16[5,4,256]{2,1,0:T(4,128)(2,1)S(1)} %get-tuple-element.24), channel_id=1, source_target_pairs={{252,0},{0,4},{4,8},{8,12},{12,16},{16,20},{20,24},{24,28},{28,32}... | collective-permute-start | bytes 30728 | tf_op jit(solution)/shard_map/ppermute | solution.py:25
  37.2 10.2 %collective-permute-start.7 = (bf16[2,5,4,256]{3,2,1,0:T(4,128)(2,1)S(1)}, bf16[2,5,4,256]{3,2,1,0:T(4,128)(2,1)S(1)}, u32[]{:S(2)}, u32[]{:S(2)}) collective-permute-start(bf16[2,5,4,256]{3,2,1,0:T(4,128)(2,1)S(1)} %pad_maximum_fusion.e0), channel_id=1, source_target_pairs={{1,0},{0,1},{3,2},{2,3},{5,4},{4,5},{7,6},{6,7},{9,8},{8,9},{11,10... | collective-permute-start | bytes 61448 | tf_op jit(solution)/shard_map/ppermute | solution.py:29
  39.2 8.2 %collective-permute-start.8 = (bf16[2,5,4,256]{3,2,1,0:T(4,128)(2,1)S(1)}, bf16[2,5,4,256]{3,2,1,0:T(4,128)(2,1)S(1)}, u32[]{:S(2)}, u32[]{:S(2)}) collective-permute-start(bf16[2,5,4,256]{3,2,1,0:T(4,128)(2,1)S(1)} %pad_maximum_fusion.e0), channel_id=1, source_target_pairs={{2,0},{3,1},{0,2},{1,3},{6,4},{7,5},{4,6},{5,7},{10,8},{11,9},{8,1... | collective-permute-start | bytes 61448 | tf_op jit(solution)/shard_map/ppermute | solution.py:29
  39.8 7.6 %collective-permute-start.9 = (bf16[2,5,4,256]{3,2,1,0:T(4,128)(2,1)S(1)}, bf16[2,5,4,256]{3,2,1,0:T(4,128)(2,1)S(1)}, u32[]{:S(2)}, u32[]{:S(2)}) collective-permute-start(bf16[2,5,4,256]{3,2,1,0:T(4,128)(2,1)S(1)} %pad_maximum_fusion.e0), channel_id=1, source_target_pairs={{3,0},{2,1},{1,2},{0,3},{7,4},{6,5},{5,6},{4,7},{11,8},{10,9},{9,1... | collective-permute-start | bytes 61448 | tf_op jit(solution)/shard_map/ppermute | solution.py:29

commit v2 on v1

--- a/solution.py
+++ b/solution.py
@@ -15,7 +15,8 @@
 UP = 8
 GR = 40
 KP = 17
-UN = 2
+UN = 8
+UF = 4
 MIB = 1024 * 1024
 DMA = pltpu.SemaphoreType.DMA
 
@@ -45,36 +46,29 @@
         ]
         for t in range(nt // ch)
     ]
-    for c in small + copies[0] + copies[1]:
+    for c in small:
         c.start()
+    for cs in copies:
+        for c in cs:
+            c.start()
     for c in small:
         c.wait()
     mcopies = [pltpu.make_async_copy(met.at[hs[s]], own.at[s], msem.at[s]) for s in range(2)]
     rcopies = [pltpu.make_async_copy(forcing.at[js[t]], rows.at[t], rsem.at[t]) for t in range(nt)]
     for c in mcopies + rcopies:
         c.start()
-    for cs in copies[2:]:
-        for c in cs:
-            c.start()
     zero = jnp.zeros((8, LN), F32)
 
     def clear(t, _):
         for b in range(nb):
-            for k in range(nk):
-                for ref in (l0, l1):
-                    ref[b, t, k, UP - 8 : UP, :] = zero
-                    ref[b, t, k, UP + ni : UP + ni + 8, :] = zero
+            for ref in (l0, l1):
+                flat = ref.at[b].reshape(nt * KP * GR, LN)
+                for row in (UP - 1, UP + ni):
+                    for k in range(0, nk, 8):
+                        flat[pl.ds((t * KP + k) * GR + row, 8, stride=GR), :] = zero
         return 0
 
     lax.fori_loop(0, nt, clear, 0)
-    for c in mcopies:
-        c.wait()
-    for out, lo, near, far in ((edge_w, 0, 0, 1), (edge_e, ni - 8, ni - 1, ni - 2)):
-        for s, f, outs in ((0, 0, ((0, near), (4, far))), (0, 1, ((1, near),)),
-                           (0, 2, ((2, near),)), (1, 0, ((3, near),))):
-            x = [own[s, f, q, lo : lo + 8, :].astype(F32) for q in range(own.shape[2])]
-            for n, c in outs:
-                out[n] = jnp.concatenate([y[c - lo : c - lo + 1] for y in x], axis=0).astype(BF)
     for cs, t0 in zip(copies, range(0, nt, ch)):
         for b in range(nb):
             cs[b].wait()
@@ -90,6 +84,14 @@
         r = rows[t].astype(F32)
         to_w[2 * nt, t] = r[0].astype(BF)
         to_e[2 * nt, t] = r[ni - 1].astype(BF)
+    for c in mcopies:
+        c.wait()
+    for out, lo, near, far in ((edge_w, 0, 0, 1), (edge_e, ni - 8, ni - 1, ni - 2)):
+        for s, f, outs in ((0, 0, ((0, near), (4, far))), (0, 1, ((1, near),)),
+                           (0, 2, ((2, near),)), (1, 0, ((3, near),))):
+            x = [own[s, f, q, lo : lo + 8, :].astype(F32) for q in range(own.shape[2])]
+            for n, c in outs:
+                out[n] = jnp.concatenate([y[c - lo : c - lo + 1] for y in x], axis=0).astype(BF)
 
 
 def pack(hour, ids, lam, met, forcing):
@@ -130,12 +132,23 @@
     return lane == 0, lane == LN - 1
 
 
-def shifted(p, o):
+def shifted(x, n, o):
     first, last = ends()
-    nb = len(p)
-    rp = [roll2(x, -1) for x in p]
-    ro = [roll2(x, 1) for x in o]
-    return [jnp.where(last, rp[(b + 1) % nb], rp[b]) + jnp.where(first, ro[(b - 1) % nb], ro[b]) for b in range(nb)]
+    nb = len(x)
+    out = []
+    for b in range(nb):
+        p = jnp.where(first, x[b + 1], x[b]) if b + 1 < nb else x[b]
+        q = jnp.where(last, x[b - 1], x[b]) if b else x[b]
+        out.append(roll2(p * n[b], -1) + roll2(q * o[b], 1))
+    return out
+
+
+def seam(n, o, first, last):
+    nb = len(n)
+    return (
+        [jnp.where(first, n[b + 1] if b + 1 < nb else 0.0, n[b]) for b in range(nb)],
+        [jnp.where(last, o[b - 1] if b else 0.0, o[b]) for b in range(nb)],
+    )
 
 
 def steps_kernel(m0, m1, m2, m3, l0, l1in, rows, res, oc, l1, co, kz):
@@ -163,20 +176,22 @@
             k = base + q
             top = jnp.where(k < nk - 1, 1.0, 0.0).astype(F32)
             for s in range(2):
-                for b in range(nb):
-                    for a in range(na):
-                        i = 8 * a
+                for a in range(na):
+                    i = 8 * a
+                    ns, os = [], []
+                    for b in range(nb):
                         cx, cy, mx = (ref[s, f, q, i : i + 8, b * LN : (b + 1) * LN].astype(F32) for f in range(3))
-                        n = jnp.maximum(cy, 0.0)
-                        o = n - cy
                         e = jnp.maximum(cx, 0.0)
-                        w = e - cx
+                        ns.append(jnp.maximum(cy, 0.0))
+                        os.append(ns[b] - cy)
                         co[s, 0, b, k, UP + i : UP + i + 8, :] = 1.0 - jnp.abs(cx) - jnp.abs(cy)
                         co[s, 1, b, k, UP + i : UP + i + 8, :] = e
-                        co[s, 2, b, k, UP + i : UP + i + 8, :] = w
-                        co[s, 3, b, k, UP + i : UP + i + 8, :] = jnp.where(first, 0.0, n) if b == 0 else n
-                        co[s, 4, b, k, UP + i : UP + i + 8, :] = jnp.where(last, 0.0, o) if b == nb - 1 else o
+                        co[s, 2, b, k, UP + i : UP + i + 8, :] = e - cx
                         kz[s, b, k + 1, i : i + 8, :] = (0.02 + 0.25 * jnp.abs(mx)) * top
+                    ns, os = seam(ns, os, first, last)
+                    for b in range(nb):
+                        co[s, 3, b, k, UP + i : UP + i + 8, :] = ns[b]
+                        co[s, 4, b, k, UP + i : UP + i + 8, :] = os[b]
             return 0
 
         lax.fori_loop(0, nl, coeffs, 0)
@@ -196,7 +211,7 @@
                      co[s, 3, b, k, r0 : r0 + 8, :], co[s, 4, b, k, r0 : r0 + 8, :]))
                 for t in range(nt):
                     x = [src[b, t, k, r0 : r0 + 8, :] for b in range(nb)]
-                    y = shifted([x[b] * c[b][5] for b in range(nb)], [x[b] * c[b][6] for b in range(nb)])
+                    y = shifted(x, [c[b][5] for b in range(nb)], [c[b][6] for b in range(nb)])
                     for b in range(nb):
                         ce, ea, we, up, dn, _, _ = c[b]
                         z = ((x[b] * ce + src[b, t, k, r0 + 1 : r0 + 9, :] * ea)
@@ -289,6 +304,7 @@
                     et[side, n, pl.ds((r ^ m) * nl + q, 1), :] = x[q : q + 1]
     for side, src in ((0, from_e), (1, from_w)):
         sg = 1.0 if side == 0 else -1.0
+        ns, os = [], []
         for b in range(nb):
             sl = slice(b * LN, (b + 1) * LN)
             hs[side, b, 0:8, :] = zero
@@ -308,18 +324,22 @@
             hc[side, 0, b, 0:nk] = 1.0 - jnp.abs(cx) - jnp.abs(cy) - ku - km
             hc[side, 1, b, 0:nk] = jnp.maximum(sg * far, 0.0)
             hc[side, 2, b, 0:nk] = oc[side, 0, b]
-            hc[side, 3, b, 0:nk] = jnp.where(lanes == 0, 0.0, n) if b == 0 else n
-            hc[side, 4, b, 0:nk] = jnp.where(lanes == LN - 1, 0.0, o) if b == nb - 1 else o
+            ns.append(n)
+            os.append(o)
             hc[side, 5, b, 0:nk] = ku
             hc[side, 6, b, 0:nk] = km
             hc[side, 7, b, 0:8] = zero
             hc[side, 7, b, 8 : 8 + nk] = jnp.maximum(sg * cx, 0.0)
             hc[side, 7, b, 8 + nk : 16 + nk] = zero
             hc[side, 8, b, 0:nk] = jnp.maximum(sg * cx1, 0.0)
+        ns, os = seam(ns, os, lanes == 0, lanes == LN - 1)
+        for b in range(nb):
+            hc[side, 3, b, 0:nk] = ns[b]
+            hc[side, 4, b, 0:nk] = os[b]
     fr = [res.at[b].reshape(nt * KP * ni, LN) for b in range(nb)]
     f0 = [l0.at[b].reshape(nt * KP * GR, LN) for b in range(nb)]
 
-    def one(t, _):
+    def one(t):
         for side, own, inner in ((0, ni - 1, ni - 2), (1, 0, 1)):
             for h in range(nk // 8):
                 k0 = 8 * h
@@ -332,8 +352,8 @@
                 dl = [[x[d][b] * e[d][b] for b in range(nb)] for d in range(3)]
                 far = [g[nt + t, k0 : k0 + 8, b * LN : (b + 1) * LN].astype(F32) for b in range(nb)]
                 mine = [f0[b][pl.ds((t * KP + k0) * GR + UP + own, 8, stride=GR), :] for b in range(nb)]
-                sh = shifted([x[1][b] * c[3][b] for b in range(nb)], [x[1][b] * c[4][b] for b in range(nb)])
-                sd = shifted([dl[1][b] * p[3][b] for b in range(nb)], [dl[1][b] * p[4][b] for b in range(nb)])
+                sh = shifted(x[1], c[3], c[4])
+                sd = shifted(dl[1], p[3], p[4])
                 for b in range(nb):
                     y = (x[1][b] * c[0][b] + far[b] * c[1][b] + mine[b] * c[2][b] + sh[b]
                          + x[2][b] * c[5][b] + x[0][b] * c[6][b])
@@ -347,9 +367,13 @@
                     fr[b][at, :] = fr[b][at, :] + dl[1][b] * p[2][b]
         for b in range(nb):
             pltpu.make_async_copy(res.at[b, t, 0:nk], out.at[t, :, :, b * LN : (b + 1) * LN], osem.at[b]).start()
+
+    def body(h, _):
+        for u in range(UF):
+            one(UF * h + u)
         return 0
 
-    lax.fori_loop(0, nt, one, 0)
+    lax.fori_loop(0, nt // UF, body, 0)
     for b in range(nb):
         pltpu.make_async_copy(res.at[b, :, 0:nk], out.at[:, :, :, b * LN : (b + 1) * LN], osem.at[b]).wait()
 
@@ -369,7 +393,8 @@
             pltpu.VMEM((2, 5, nk, nb * LN), F32),
             DMA((nb,)),
         ],
-        compiler_params=pltpu.CompilerParams(vmem_limit_bytes=16 * MIB),
+        compiler_params=pltpu.CompilerParams(
+            vmem_limit_bytes=12 * MIB),
         cost_estimate=pl.CostEstimate(flops=10**6, bytes_accessed=8 * MIB, transcendentals=0),
         name="finish",
     )(res, l0, oc, from_w, from_e, *es)

time: 50.4 us -> 48.6 us (0.964)
  Pallas kernels: 12.5 us -> 10.7 us
    pallas_call x1, Pallas kernels: 6.47 us -> 5.57 us  [steps(): pl.pallas_call(steps_kernel, out_shape=[pltpu.VMEM((nb, nt, KP, ni, LN),...]
  transfers between devices with their start and end apart: 10 -> 10, of which waited for: 2 -> 2; matrix products, arithmetic and copies ran while one was open for 0% -> 0% of each run, Pallas kernels for 13% -> 11%
where the time goes in v2:
time: 48.6 us; the launch traced here: 48.5 us
  starting transfers between devices  28.3 us (58%)
  Pallas kernels  10.7 us (22%)
  waiting for transfers between devices  9.42 us (19%)
    ppermute x4, starting transfers between devices, passed_along(): lax.ppermute(block, axis, [((i - distance) % n, i) for i in range(n)])  21.1 us
    ppermute x4, waiting for transfers between devices, passed_along(): lax.ppermute(block, axis, [((i - distance) % n, i) for i in range(n)])  9.41 us
    ppermute x6, starting transfers between devices, swapped(): lax.ppermute(block, axis, [(i ^ bit, i) for i in range(lax.axis_size(axis...  7.11 us
    pallas_call x1, Pallas kernels, steps(): pl.pallas_call(steps_kernel, out_shape=[pltpu.VMEM((nb, nt, KP, ni, LN),...  5.57 us
    pallas_call x1, Pallas kernels, pack(): pl.pallas_call(pack_kernel, out_shape=[jax.ShapeDtypeStruct((2,) + met.sh...  2.82 us
    pallas_call x1, Pallas kernels, finish(): pl.pallas_call(finish_kernel, out_shape=jax.ShapeDtypeStruct((nt, nk, ni,...  2.32 us
  transfers between devices with their start and end apart: 10, of which 2 were waited for; matrix products, arithmetic and copies ran while one was open for 0% of the time, Pallas kernels for 11%

profile of v2, /device:TPU:1, one launch (start us, length us, event | category | flops | bytes accessed | tf_op | source)
XLA Modules:
  0.0 48.5 jit_solution(1538108101760407807)
XLA Ops:
  0.0 2.8 %pack.1 = (bf16[2,3,4,16,256]{4,3,2,1,0:T(8,128)(2,1)S(1)}, bf16[33,16,256]{2,1,0:T(8,128)(2,1)S(1)}, bf16[33,16,256]{2,1,0:T(8,128)(2,1)S(1)}, bf16[5,4,256]{2,...) custom-call(s32[2]{0:T(128)} %hour.1, s32[16]{0:T(128)} %ids.1, ...), custom_call_target="tpu_custom_call" | custom-call | flops 1000000 | bytes 10485760 | tf_op jit(solution)/shard_map/pack/pallas_call | solution.py:102
  2.8 2.1 %collective-permute-start.1 = (bf16[2,3,4,16,256]{4,3,2,1,0:T(8,128)(2,1)S(1)}, bf16[2,3,4,16,256]{4,3,2,1,0:T(8,128)(2,1)S(1)}, u32[]{:S(2)}, u32[]{:S(2)}) collective-permute-start(bf16[2,3,4,16,256]{4,3,2,1,0:T(8,128)(2,1)S(1)} %get-tuple-element.15.m0), channel_id=1, source_target_pairs={{2,0},{3,1},{0,2},{1,3},{6,4},{7,5},{4,6},{5,7},{10,8},{11,9},{8,1... | collective-permute-start | bytes 589832 | tf_op jit(solution)/shard_map/ppermute | solution.py:30
  4.9 1.6 %collective-permute-start.3 = (bf16[33,16,256]{2,1,0:T(8,128)(2,1)S(1)}, bf16[33,16,256]{2,1,0:T(8,128)(2,1)S(1)}, u32[]{:S(2)}, u32[]{:S(2)}) collective-permute-start(bf16[33,16,256]{2,1,0:T(8,128)(2,1)S(1)} %get-tuple-element.21), channel_id=1, source_target_pairs={{252,0},{0,4},{4,8},{8,12},{12,16},{16,20},{20,24},{24,28},{28,32}... | collective-permute-start | bytes 811016 | tf_op jit(solution)/shard_map/ppermute | solution.py:26
  6.6 8.6 %collective-permute-start.4 = (bf16[33,16,256]{2,1,0:T(8,128)(2,1)S(1)}, bf16[33,16,256]{2,1,0:T(8,128)(2,1)S(1)}, u32[]{:S(2)}, u32[]{:S(2)}) collective-permute-start(bf16[33,16,256]{2,1,0:T(8,128)(2,1)S(1)} %get-tuple-element.22), channel_id=1, source_target_pairs={{4,0},{8,4},{12,8},{16,12},{20,16},{24,20},{28,24},{32,28},{36,32}... | collective-permute-start | bytes 811016 | tf_op jit(solution)/shard_map/ppermute | solution.py:26
  15.1 1.2 %collective-permute-start = (bf16[2,3,4,16,256]{4,3,2,1,0:T(8,128)(2,1)S(1)}, bf16[2,3,4,16,256]{4,3,2,1,0:T(8,128)(2,1)S(1)}, u32[]{:S(2)}, u32[]{:S(2)}) collective-permute-start(bf16[2,3,4,16,256]{4,3,2,1,0:T(8,128)(2,1)S(1)} %get-tuple-element.15.m0), channel_id=1, source_target_pairs={{1,0},{0,1},{3,2},{2,3},{5,4},{4,5},{7,6},{6,7},{9,8},{8,9},{11,10... | collective-permute-start | bytes 589832 | tf_op jit(solution)/shard_map/ppermute | solution.py:30
  16.4 0.0 collective-permute-done.1.m2
  16.4 0.0 collective-permute-start.2
  16.4 10.9 %collective-permute-start.5 = (bf16[5,4,256]{2,1,0:T(4,128)(2,1)S(1)}, bf16[5,4,256]{2,1,0:T(4,128)(2,1)S(1)}, u32[]{:S(2)}, u32[]{:S(2)}) collective-permute-start(bf16[5,4,256]{2,1,0:T(4,128)(2,1)S(1)} %get-tuple-element.23), channel_id=1, source_target_pairs={{4,0},{8,4},{12,8},{16,12},{20,16},{24,20},{28,24},{32,28},{36,32}... | collective-permute-start | bytes 30728 | tf_op jit(solution)/shard_map/ppermute | solution.py:26
  27.3 0.8 %collective-permute-done.5 = bf16[5,4,256]{2,1,0:T(4,128)(2,1)S(1)} collective-permute-done((bf16[5,4,256]{2,1,0:T(4,128)(2,1)S(1)}, bf16[5,4,256]{2,1,0:T(4,128)(2,1)S(1)}, u32[]{:S(2)}, u32[]{:S(2)}) %collective-permute-start.5) | collective-permute-done | bytes 10272 | tf_op jit(solution)/shard_map/ppermute | solution.py:26
  28.1 0.0 collective-permute-start.6
  28.1 8.6 %collective-permute-done.6 = bf16[5,4,256]{2,1,0:T(4,128)(2,1)S(1)} collective-permute-done((bf16[5,4,256]{2,1,0:T(4,128)(2,1)S(1)}, bf16[5,4,256]{2,1,0:T(4,128)(2,1)S(1)}, u32[]{:S(2)}, u32[]{:S(2)}) %collective-permute-start.6) | collective-permute-done | bytes 10272 | tf_op jit(solution)/shard_map/ppermute | solution.py:26
  36.8 2.0 %collective-permute-start.7 = (bf16[2,5,4,256]{3,2,1,0:T(4,128)(2,1)S(1)}, bf16[2,5,4,256]{3,2,1,0:T(4,128)(2,1)S(1)}, u32[]{:S(2)}, u32[]{:S(2)}) collective-permute-start(bf16[2,5,4,256]{3,2,1,0:T(4,128)(2,1)S(1)} %pad_maximum_fusion.e0), channel_id=1, source_target_pairs={{1,0},{0,1},{3,2},{2,3},{5,4},{4,5},{7,6},{6,7},{9,8},{8,9},{11,10... | collective-permute-start | bytes 61448 | tf_op jit(solution)/shard_map/ppermute | solution.py:30
  38.8 0.0 collective-permute-done.m1
  38.8 0.6 %collective-permute-start.8 = (bf16[2,5,4,256]{3,2,1,0:T(4,128)(2,1)S(1)}, bf16[2,5,4,256]{3,2,1,0:T(4,128)(2,1)S(1)}, u32[]{:S(2)}, u32[]{:S(2)}) collective-permute-start(bf16[2,5,4,256]{3,2,1,0:T(4,128)(2,1)S(1)} %pad_maximum_fusion.e0), channel_id=1, source_target_pairs={{2,0},{3,1},{0,2},{1,3},{6,4},{7,5},{4,6},{5,7},{10,8},{11,9},{8,1... | collective-permute-start | bytes 61448 | tf_op jit(solution)/shard_map/ppermute | solution.py:30
  39.4 0.0 collective-permute-done.2.m3
  39.4 1.1 %collective-permute-start.9 = (bf16[2,5,4,256]{3,2,1,0:T(4,128)(2,1)S(1)}, bf16[2,5,4,256]{3,2,1,0:T(4,128)(2,1)S(1)}, u32[]{:S(2)}, u32[]{:S(2)}) collective-permute-start(bf16[2,5,4,256]{3,2,1,0:T(4,128)(2,1)S(1)} %pad_maximum_fusion.e0), channel_id=1, source_target_pairs={{3,0},{2,1},{1,2},{0,3},{7,4},{6,5},{5,6},{4,7},{11,8},{10,9},{9,1... | collective-permute-start | bytes 61448 | tf_op jit(solution)/shard_map/ppermute | solution.py:30
  40.5 5.6 %steps.1 = (f32[2,16,17,16,128]{4,3,2,1,0:T(8,128)S(1)}, f32[2,7,2,16,128]{4,3,2,1,0:T(8,128)S(1)}, f32[2,16,17,40,128]{4,3,2,1,0:T(8,128)S(1)}) custom-call(bf16[2,3,4,16,256]{4,3,2,1,0:T(8,128)(2,1)S(1)} %get-tuple-element.15.m0, bf16[2,3,4,16,256]{4,3,2,1,0:T(8,128)(2,1)S(1)} %collective-permute-done.m1, ...), custom_call_target="tpu_custom_call", output_to_operand_aliasing={{2}: (5, {})} | custom-call | flops 40000000 | bytes 20971520 | tf_op jit(solution)/shard_map/steps/pallas_call | solution.py:270
  46.1 0.0 collective-permute-done.7.e1
  46.1 0.0 collective-permute-done.8.e2
  46.1 0.0 collective-permute-done.9.e3
  46.1 0.0 collective-permute-done.3.from_w
  46.1 0.0 collective-permute-done.4.from_e
  46.1 2.3 %finish.1 = f32[16,16,16,256]{3,2,1,0:T(8,128)} custom-call(f32[2,16,17,16,128]{4,3,2,1,0:T(8,128)S(1)} %get-tuple-element.19.res, f32[2,16,17,40,128]{4,3,2,1,0:T(8,128)S(1)} %get-tuple-element.16.l0, f32[2,7,2,16,128]{4,3,2,1,0:T(8,128)S(1)} %get-tuple-element.20.oc, bf16[33,16,256]{2,1,0:T(8,128)(2,1)S(1)} %collective-permute-done.3.from_w, ...), custom_call_target="tpu_custom_call" | custom-call | flops 1000000 | bytes 8388608 | tf_op jit(solution)/shard_map/finish/pallas_call | solution.py:384
  (1 shorter events, 0.0 us)
Async XLA Ops:
  2.8 13.6 %collective-permute-start.1 = (bf16[2,3,4,16,256]{4,3,2,1,0:T(8,128)(2,1)S(1)}, bf16[2,3,4,16,256]{4,3,2,1,0:T(8,128)(2,1)S(1)}, u32[]{:S(2)}, u32[]{:S(2)}) collective-permute-start(bf16[2,3,4,16,256]{4,3,2,1,0:T(8,128)(2,1)S(1)} %get-tuple-element.15.m0), channel_id=1, source_target_pairs={{2,0},{3,1},{0,2},{1,3},{6,4},{7,5},{4,6},{5,7},{10,8},{11,9},{8,1... | collective-permute-start | bytes 589832 | tf_op jit(solution)/shard_map/ppermute | solution.py:30
  4.9 41.2 %collective-permute-start.3 = (bf16[33,16,256]{2,1,0:T(8,128)(2,1)S(1)}, bf16[33,16,256]{2,1,0:T(8,128)(2,1)S(1)}, u32[]{:S(2)}, u32[]{:S(2)}) collective-permute-start(bf16[33,16,256]{2,1,0:T(8,128)(2,1)S(1)} %get-tuple-element.21), channel_id=1, source_target_pairs={{252,0},{0,4},{4,8},{8,12},{12,16},{16,20},{20,24},{24,28},{28,32}... | collective-permute-start | bytes 811016 | tf_op jit(solution)/shard_map/ppermute | solution.py:26
  6.6 39.6 %collective-permute-start.4 = (bf16[33,16,256]{2,1,0:T(8,128)(2,1)S(1)}, bf16[33,16,256]{2,1,0:T(8,128)(2,1)S(1)}, u32[]{:S(2)}, u32[]{:S(2)}) collective-permute-start(bf16[33,16,256]{2,1,0:T(8,128)(2,1)S(1)} %get-tuple-element.22), channel_id=1, source_target_pairs={{4,0},{8,4},{12,8},{16,12},{20,16},{24,20},{28,24},{32,28},{36,32}... | collective-permute-start | bytes 811016 | tf_op jit(solution)/shard_map/ppermute | solution.py:26
  15.1 23.6 %collective-permute-start = (bf16[2,3,4,16,256]{4,3,2,1,0:T(8,128)(2,1)S(1)}, bf16[2,3,4,16,256]{4,3,2,1,0:T(8,128)(2,1)S(1)}, u32[]{:S(2)}, u32[]{:S(2)}) collective-permute-start(bf16[2,3,4,16,256]{4,3,2,1,0:T(8,128)(2,1)S(1)} %get-tuple-element.15.m0), channel_id=1, source_target_pairs={{1,0},{0,1},{3,2},{2,3},{5,4},{4,5},{7,6},{6,7},{9,8},{8,9},{11,10... | collective-permute-start | bytes 589832 | tf_op jit(solution)/shard_map/ppermute | solution.py:30
  16.4 23.0 %collective-permute-start.2 = (bf16[2,3,4,16,256]{4,3,2,1,0:T(8,128)(2,1)S(1)}, bf16[2,3,4,16,256]{4,3,2,1,0:T(8,128)(2,1)S(1)}, u32[]{:S(2)}, u32[]{:S(2)}) collective-permute-start(bf16[2,3,4,16,256]{4,3,2,1,0:T(8,128)(2,1)S(1)} %collective-permute-done.1.m2), channel_id=1, source_target_pairs={{1,0},{0,1},{3,2},{2,3},{5,4},{4,5},{7,6},{6,7},{9,8},{8,9},{11,10... | collective-permute-start | bytes 589832 | tf_op jit(solution)/shard_map/ppermute | solution.py:30
  16.4 11.8 %collective-permute-start.5 = (bf16[5,4,256]{2,1,0:T(4,128)(2,1)S(1)}, bf16[5,4,256]{2,1,0:T(4,128)(2,1)S(1)}, u32[]{:S(2)}, u32[]{:S(2)}) collective-permute-start(bf16[5,4,256]{2,1,0:T(4,128)(2,1)S(1)} %get-tuple-element.23), channel_id=1, source_target_pairs={{4,0},{8,4},{12,8},{16,12},{20,16},{24,20},{28,24},{32,28},{36,32}... | collective-permute-start | bytes 30728 | tf_op jit(solution)/shard_map/ppermute | solution.py:26
  28.1 8.6 %collective-permute-start.6 = (bf16[5,4,256]{2,1,0:T(4,128)(2,1)S(1)}, bf16[5,4,256]{2,1,0:T(4,128)(2,1)S(1)}, u32[]{:S(2)}, u32[]{:S(2)}) collective-permute-start(bf16[5,4,256]{2,1,0:T(4,128)(2,1)S(1)} %get-tuple-element.24), channel_id=1, source_target_pairs={{252,0},{0,4},{4,8},{8,12},{12,16},{16,20},{20,24},{24,28},{28,32}... | collective-permute-start | bytes 30728 | tf_op jit(solution)/shard_map/ppermute | solution.py:26
  36.8 9.3 %collective-permute-start.7 = (bf16[2,5,4,256]{3,2,1,0:T(4,128)(2,1)S(1)}, bf16[2,5,4,256]{3,2,1,0:T(4,128)(2,1)S(1)}, u32[]{:S(2)}, u32[]{:S(2)}) collective-permute-start(bf16[2,5,4,256]{3,2,1,0:T(4,128)(2,1)S(1)} %pad_maximum_fusion.e0), channel_id=1, source_target_pairs={{1,0},{0,1},{3,2},{2,3},{5,4},{4,5},{7,6},{6,7},{9,8},{8,9},{11,10... | collective-permute-start | bytes 61448 | tf_op jit(solution)/shard_map/ppermute | solution.py:30
  38.8 7.3 %collective-permute-start.8 = (bf16[2,5,4,256]{3,2,1,0:T(4,128)(2,1)S(1)}, bf16[2,5,4,256]{3,2,1,0:T(4,128)(2,1)S(1)}, u32[]{:S(2)}, u32[]{:S(2)}) collective-permute-start(bf16[2,5,4,256]{3,2,1,0:T(4,128)(2,1)S(1)} %pad_maximum_fusion.e0), channel_id=1, source_target_pairs={{2,0},{3,1},{0,2},{1,3},{6,4},{7,5},{4,6},{5,7},{10,8},{11,9},{8,1... | collective-permute-start | bytes 61448 | tf_op jit(solution)/shard_map/ppermute | solution.py:30
  39.4 6.7 %collective-permute-start.9 = (bf16[2,5,4,256]{3,2,1,0:T(4,128)(2,1)S(1)}, bf16[2,5,4,256]{3,2,1,0:T(4,128)(2,1)S(1)}, u32[]{:S(2)}, u32[]{:S(2)}) collective-permute-start(bf16[2,5,4,256]{3,2,1,0:T(4,128)(2,1)S(1)} %pad_maximum_fusion.e0), channel_id=1, source_target_pairs={{3,0},{2,1},{1,2},{0,3},{7,4},{6,5},{5,6},{4,7},{11,8},{10,9},{9,1... | collective-permute-start | bytes 61448 | tf_op jit(solution)/shard_map/ppermute | solution.py:30
